TPU v7x, 128 devices: a whole 4x4x4 slice. The times are simulated.
128 devices in a mesh: dev: 32 (over z, x, core), rep: 4 (over y).
Axes of the slice: x: 4, y: 4, z: 4, core: 2. Of those that a mesh axis runs over, the one named last changes fastest.
Arguments:
- activations: bfloat16 [4, 256, 64, 2048], P('rep', 'dev'), may hold values from -6 to 6
- out_grads: bfloat16 [4, 256, 64, 1024], P('rep', 'dev'), may hold values from -6 to 6
- inverse: float32 [32, 2048, 2048], P('dev'), may hold values from -4 to 11, as said below
Outputs:
- whitened: float32 [4, 256, 65536], P('rep', 'dev')
- leverage: float32 [4, 256], P('rep', 'dev')
- new_inverse: float32 [32, 2048, 2048], P('dev', 'rep')
Inputs may be any that keep to these rules, and one draw needn't show every extreme that they name: Each 2048 x 2048 matrix of inverse is symmetric positive definite.
All inputs are finite; a program needn't handle non-finite values.
Results may differ from a plain program's by a relative error of at most 0.0003.
Values sent between devices are 32-bit elements; how exact they have to be, the bound alone decides.
No kernel may reach another device: no remote copies, remote signals or barrier semaphores. Data moves between devices by JAX's collectives and lax.ppermute only.
A program may use at most 128 MiB of HBM per device.

v0:
```python
import jax
import jax.numpy as jnp
from jax import lax
from jax.sharding import PartitionSpec as P

KI = 64
KO = 32


def body(activations, out_grads, inverse):
    num_dev = lax.axis_size("dev")
    num_rep = lax.axis_size("rep")
    examples = activations.shape[1]
    tokens = activations.shape[2]
    feat_width = KI * KO
    group_rows = examples * num_dev
    acts_four = activations.reshape(examples, tokens, num_dev, KI)
    grads_four = out_grads.reshape(examples, tokens, num_dev, KO)
    features = jnp.einsum(
        "etmo,etmi->emoi", grads_four, acts_four, preferred_element_type=jnp.float32
    )
    features = features.reshape(examples, num_dev, feat_width) * tokens ** (-0.5)
    moved = lax.all_to_all(features, "dev", split_axis=1, concat_axis=0, tiled=True)
    own_rows = moved[:, 0, :]
    module_inverse = inverse[0]
    whitened = jnp.dot(own_rows, module_inverse, precision=lax.Precision.HIGHEST)
    lev_terms = jnp.sum(own_rows * whitened, axis=1)
    lev_send = lax.psum(lev_terms, "dev") / (num_dev * feat_width)
    all_rows, all_white, all_lev = (
        lax.all_gather(own_rows, "rep", axis=0, tiled=True),
        lax.all_gather(whitened, "rep", axis=0, tiled=True),
        lax.all_gather(lev_send, "rep", axis=0, tiled=True),
    )
    damping = 1.0 + feat_width * all_lev
    capacitance = jnp.dot(all_rows, all_white.T, precision=lax.Precision.HIGHEST) + jnp.diag(
        damping
    )
    cholesky_factor = jnp.linalg.cholesky(capacitance)
    row_count = feat_width // num_rep
    first_row = lax.axis_index("rep") * row_count
    white_block = lax.dynamic_slice_in_dim(all_white, first_row, row_count, 1)
    solved = jax.scipy.linalg.cho_solve((cholesky_factor, True), white_block)
    inverse_rows = lax.dynamic_slice_in_dim(module_inverse, first_row, row_count, 0)
    updated = inverse_rows - jnp.dot(solved.T, all_white, precision=lax.Precision.HIGHEST)
    returned = lax.all_to_all(
        whitened.reshape(num_dev, examples, 1, feat_width),
        "dev",
        split_axis=0,
        concat_axis=2,
        tiled=True,
    )
    whitened_out = returned.reshape(1, examples, num_dev * feat_width)
    lev_first = lax.axis_index("rep") * group_rows + lax.axis_index("dev") * examples
    lev_out = lax.dynamic_slice_in_dim(all_lev, lev_first, examples, 0).reshape(1, examples)
    return (whitened_out, lev_out, updated.reshape(1, row_count, feat_width))


def solution(mesh):
    in_specs = (P("rep", "dev", None, None), P("rep", "dev", None, None), P("dev", None, None))
    out_specs = (P("rep", "dev", None), P("rep", "dev"), P("dev", "rep", None))
    return jax.shard_map(body, mesh=mesh, in_specs=in_specs, out_specs=out_specs, check_vma=False)
```

profile of v0, /device:TPU:1, one launch (start us, length us, event | category | flops | bytes accessed | tf_op | source)
XLA Modules:
  0.0 655.6 jit_solution(12305604017612134976)
XLA Ops:
  26.8 37.5 %all_to_all.30 = f32[8,32,2048]{2,0,1:T(8,128)S(1)} all-to-all(f32[8,32,2048]{2,0,1:T(8,128)S(1)} %copy.16), channel_id=1, replica_groups=mesh['dev'=32,'rep'=4] {'dev'}, dimensions={1} | all-to-all | bytes 4194304 | tf_op jit(solution)/shard_map/all_to_all | solution.py:23
  64.3 18.8 %multiply_reduce_fusion = (f32[256]{0:T(256)S(1)}, f32[256,2048]{1,0:T(8,128)}) fusion(f32[8,32,2048]{2,0,1:T(8,128)S(1)} %all_to_all.30, f32[1,2048,2048]{2,1,0:T(8,128)} %param.5), kind=kOutput, calls=%fused_computation.16 | convolution fusion | flops 12885950464 | bytes 20972544 | tf_op jit(solution)/shard_map/dot_general | solution.py:26
  88.0 81.7 %psum.7 = f32[256]{0:T(256)S(1)} all-reduce(f32[256]{0:T(256)S(1)} %get-tuple-element.60), channel_id=1, replica_groups=mesh['dev'=32,'rep'=4] {'dev'}, use_global_device_ids=true, to_apply=%region_1.0 | all-reduce | flops 256 | bytes 2048 | tf_op jit(solution)/shard_map/psum | solution.py:28
  169.7 8.2 %all-gather = f32[4,1,256]{2,1,0:T(1,128)S(1)} all-gather(f32[1,1,256]{2,1,0:T(1,128)S(1)} %bitcast.179), channel_id=1, replica_groups=mesh['dev'=32,'rep'=4] {'rep'}, dimensions={0}, use_global_device_ids=true | all-gather | bytes 5120 | tf_op jit(solution)/shard_map/all_gather | solution.py:32
  178.5 71.6 %all-gather.4.cloned.1.call-done = f32[1024,2048]{1,0:T(8,128)} async-done(((f32[256,2048]{1,0:T(8,128)}), f32[1024,2048]{1,0:T(8,128)}) %all-gather.4.cloned.1.call-update) | async-done | bytes 8388624 | tf_op jit(solution)/shard_map/all_gather | solution.py:30
  250.1 32.1 %fusion.106 = f32[1024,1024]{1,0:T(8,128)} fusion(f32[1024,2048]{1,0:T(8,128)} %all-gather.4.cloned.1.call-done, f32[1024,2048]{1,0:T(8,128)} %all-gather.6.cloned.1.call-done), kind=kOutput, calls=%fused_computation.229 | convolution fusion | flops 25769803776 | bytes 20971520 | tf_op jit(solution)/shard_map/dot_general | solution.py:35
  294.4 11.7 %cholesky.222 = f32[128,128]{1,0:T(8,128)S(1)} custom-call(f32[128,128]{1,0:T(8,128)S(1)} %cholesky.577), custom_call_target="Cholesky" | custom-call | tf_op jit(solution)/shard_map/jit(cholesky)/cholesky | solution.py:38
  308.7 9.8 %custom-call.66 = f32[1,128,128]{1,2,0:T(8,128)S(1)} custom-call(f32[1,128,128]{2,1,0:T(8,128)S(1)} %get-tuple-element.59), custom_call_target="InvertDiagBlocksLowerTriangular" | custom-call | tf_op jit(solution)/shard_map/jit(cholesky)/cholesky | solution.py:38
  322.4 11.8 %cholesky.243 = f32[128,128]{1,0:T(8,128)S(1)} custom-call(f32[128,128]{1,0:T(8,128)S(1)} %cholesky.581), custom_call_target="Cholesky" | custom-call | tf_op jit(solution)/shard_map/jit(cholesky)/cholesky | solution.py:38
  334.9 9.8 %custom-call.67 = f32[1,128,128]{1,2,0:T(8,128)S(1)} custom-call(f32[1,128,128]{2,1,0:T(8,128)S(1)} %get-tuple-element.56), custom_call_target="InvertDiagBlocksLowerTriangular" | custom-call | tf_op jit(solution)/shard_map/jit(cholesky)/cholesky | solution.py:38
  348.1 11.7 %cholesky.466 = f32[128,128]{1,0:T(8,128)S(1)} custom-call(f32[128,128]{1,0:T(8,128)S(1)} %cholesky.586), custom_call_target="Cholesky" | custom-call | tf_op jit(solution)/shard_map/jit(cholesky)/cholesky | solution.py:38
  360.4 9.8 %custom-call.68 = f32[1,128,128]{1,2,0:T(8,128)S(1)} custom-call(f32[1,128,128]{2,1,0:T(8,128)S(1)} %get-tuple-element.53), custom_call_target="InvertDiagBlocksLowerTriangular" | custom-call | tf_op jit(solution)/shard_map/jit(cholesky)/cholesky | solution.py:38
  373.7 11.9 %cholesky.485 = f32[128,128]{1,0:T(8,128)S(1)} custom-call(f32[128,128]{1,0:T(8,128)S(1)} %cholesky.591), custom_call_target="Cholesky" | custom-call | tf_op jit(solution)/shard_map/jit(cholesky)/cholesky | solution.py:38
  386.3 9.8 %custom-call.69 = f32[1,128,128]{1,2,0:T(8,128)S(1)} custom-call(f32[1,128,128]{2,1,0:T(8,128)S(1)} %get-tuple-element.50), custom_call_target="InvertDiagBlocksLowerTriangular" | custom-call | tf_op jit(solution)/shard_map/jit(cholesky)/cholesky | solution.py:38
  399.5 11.7 %cholesky.504 = f32[128,128]{1,0:T(8,128)S(1)} custom-call(f32[128,128]{1,0:T(8,128)S(1)} %cholesky.596), custom_call_target="Cholesky" | custom-call | tf_op jit(solution)/shard_map/jit(cholesky)/cholesky | solution.py:38
  411.9 10.2 %custom-call.70 = f32[1,128,128]{1,2,0:T(8,128)S(1)} custom-call(f32[1,128,128]{2,1,0:T(8,128)S(1)} %get-tuple-element.47), custom_call_target="InvertDiagBlocksLowerTriangular" | custom-call | tf_op jit(solution)/shard_map/jit(cholesky)/cholesky | solution.py:38
  425.3 11.7 %cholesky.524 = f32[128,128]{1,0:T(8,128)S(1)} custom-call(f32[128,128]{1,0:T(8,128)S(1)} %cholesky.601), custom_call_target="Cholesky" | custom-call | tf_op jit(solution)/shard_map/jit(cholesky)/cholesky | solution.py:38
  437.7 9.8 %custom-call.71 = f32[1,128,128]{1,2,0:T(8,128)S(1)} custom-call(f32[1,128,128]{2,1,0:T(8,128)S(1)} %get-tuple-element.44), custom_call_target="InvertDiagBlocksLowerTriangular" | custom-call | tf_op jit(solution)/shard_map/jit(cholesky)/cholesky | solution.py:38
  450.5 11.9 %cholesky.544 = f32[128,128]{1,0:T(8,128)S(1)} custom-call(f32[128,128]{1,0:T(8,128)S(1)} %cholesky.606), custom_call_target="Cholesky" | custom-call | tf_op jit(solution)/shard_map/jit(cholesky)/cholesky | solution.py:38
  463.0 9.8 %custom-call.72 = f32[1,128,128]{1,2,0:T(8,128)S(1)} custom-call(f32[1,128,128]{2,1,0:T(8,128)S(1)} %get-tuple-element.41), custom_call_target="InvertDiagBlocksLowerTriangular" | custom-call | tf_op jit(solution)/shard_map/jit(cholesky)/cholesky | solution.py:38
  475.5 11.7 %cholesky.562 = f32[128,128]{1,0:T(8,128)S(1)} custom-call(f32[128,128]{1,0:T(8,128)S(1)} %convolution_subtract_fusion.20), custom_call_target="Cholesky" | custom-call | tf_op jit(solution)/shard_map/jit(cholesky)/cholesky | solution.py:38
  502.1 22.6 %while.1 = (s32[]{:T(128)}, f32[1024,1024]{1,0:T(8,128)}, s32[8,2]{0,1:T(2,128)S(1)}, f32[8,128,128]{2,1,0:T(8,128)S(1)}, s32[]{:T(128)}) while((s32[]{:T(128)}, f32[1024,1024]{1,0:T(8,128)}, s32[8,2]{0,1:T(2,128)S(1)}, f32[8,128,128]{2,1,0:T(8,128)S(1)}, s32[]{:T(128)}) %tuple.61), condition=%wide.while_cond, body=%wide.while_body.sunk | while | flops 2 | bytes 131189 | solution.py:42
  524.7 78.8 %custom-call.73 = f32[8,128,128]{1,2,0:T(8,128)S(1)} custom-call(f32[8,128,128]{2,1,0:T(8,128)S(1)} %get-tuple-element.10), custom_call_target="InvertDiagBlocksLowerTriangular" | custom-call | tf_op jit(solution)/shard_map/jit(_cho_solve)/triangular_solve | solution.py:42
  630.3 16.7 %fusion.4 = f32[1,512,2048]{2,1,0:T(8,128)} fusion(f32[1,2048,2048]{2,1,0:T(8,128)} %param.5, s32[]{:T(128)S(6)} %select_n.20, f32[1024,512]{1,0:T(8,128)S(1)} %constant_dynamic-update-slice_fusion.36, f32[1024,2048]{1,0:T(8,128)S(1)} %bitcast.174), kind=kOutput, calls=%fused_computation.9 | convolution fusion | flops 12885950464 | bytes 18874372 | tf_op jit(solution)/shard_map/dot_general | solution.py:44
  (146 shorter events, 126.6 us)
Async XLA Ops:
  7.2 171.3 %all-gather.6.cloned.1.call-start = ((), (), s32[]{:S(2)}) async-start(), calls=%async_computation.3 | async-start | bytes 10485760 | tf_op jit(solution)/shard_map/all_gather | solution.py:31
  64.3 18.8 %copy-start = (f32[8,32,2048]{2,0,1:T(8,128)}, f32[8,32,2048]{2,0,1:T(8,128)S(1)}, u32[]{:S(2)}) copy-start(f32[8,32,2048]{2,0,1:T(8,128)S(1)} %all_to_all.30) | copy-start | bytes 6291460
  83.1 167.0 %all-gather.4.cloned.1.call-start = ((), (), s32[]{:S(2)}) async-start(), calls=%async_computation.2 | async-start | bytes 10485760 | tf_op jit(solution)/shard_map/all_gather | solution.py:30
  83.8 94.6 %all-to-all-start.1 = ((f32[32,8,1,2048]{3,1,2,0:T(8,128)}), f32[32,8,1,2048]{3,1,2,0:T(8,128)S(1)}, u32[]{:S(2)}, u32[]{:S(2)}) async-start(f32[32,8,1,2048]{3,1,2,0:T(8,128)} %bitcast.6), calls=%async_computation.1 | async-start | bytes 4194304 | tf_op jit(solution)/shard_map/all_to_all | solution.py:45
  292.5 2.0 copy-start.2
  604.9 3.9 copy-start.1
  626.3 3.6 slice-start
  628.0 2.3 slice-start.1
Sparse Core Ops, SparseCore 0:
  83.2 80.5 all-gather.5
  166.0 84.0 all-gather.3
where the time goes:
time: 664 us; the launch traced here: 656 us
  other arithmetic  260 us (39%)
  blocking collectives  127 us (19%)
  matrix products  121 us (18%)
  waiting for transfers between devices  72.4 us (11%)
  local copies, waits for them, and re-layouts  49.4 us (7%)
  between operations  20.3 us (3%)
    another operation x30, other arithmetic, body(): cholesky_factor = jnp.linalg.cholesky(capacitance)  172 us
    another operation x3, other arithmetic, body(): solved = jax.scipy.linalg.cho_solve((cholesky_factor, True), white_block)  83.7 us
    psum x1, blocking collectives, body(): lev_send = lax.psum(lev_terms, 'dev') / (num_dev * feat_width)  81.7 us
    all_gather x1, waiting for transfers between devices, body(): lax.all_gather(own_rows, 'rep', axis=0, tiled=True)  71.6 us
    all_to_all x1, blocking collectives, body(): lax.all_to_all(features, 'dev', split_axis=1, concat_axis=0, tiled=True)  37.5 us
    dot_general x1, matrix products, body(): jnp.dot(all_rows, all_white.T, precision=lax.Precision.HIGHEST)  32.1 us
    another operation x30, matrix products, body(): solved = jax.scipy.linalg.cho_solve((cholesky_factor, True), white_block)  25.2 us
    another operation x14, matrix products, body(): cholesky_factor = jnp.linalg.cholesky(capacitance)  22.9 us
  transfers between devices with their start and end apart: 3, of which 1 were waited for; matrix products, arithmetic and copies ran while one was open for 0% of the time, Pallas kernels for 0%

commit v1 on v0

--- a/solution.py
+++ b/solution.py
@@ -20,7 +20,10 @@
         "etmo,etmi->emoi", grads_four, acts_four, preferred_element_type=jnp.float32
     )
     features = features.reshape(examples, num_dev, feat_width) * tokens ** (-0.5)
-    moved = lax.all_to_all(features, "dev", split_axis=1, concat_axis=0, tiled=True)
+    moved = jnp.concatenate(
+        lax.all_to_all(jnp.stack(jnp.split(features, lax.axis_size("dev"), axis=1)), "dev", 0, 0),
+        axis=0,
+    )
     own_rows = moved[:, 0, :]
     module_inverse = inverse[0]
     whitened = jnp.dot(own_rows, module_inverse, precision=lax.Precision.HIGHEST)

time: 664 us -> 668 us (level)
    another operation x24 -> x25, local copies, waits for them, and re-layouts: 22.4 us -> 22.5 us
where the time goes in v1:
time: 668 us; the launch traced here: 658 us
  other arithmetic  260 us (39%)
  blocking collectives  127 us (19%)
  matrix products  122 us (18%)
  waiting for transfers between devices  70.2 us (11%)
  local copies, waits for them, and re-layouts  52.5 us (8%)
  between operations  20.5 us (3%)
    another operation x30, other arithmetic, body(): cholesky_factor = jnp.linalg.cholesky(capacitance)  172 us
    another operation x3, other arithmetic, body(): solved = jax.scipy.linalg.cho_solve((cholesky_factor, True), white_block)  83.7 us
    psum x1, blocking collectives, body(): lev_send = lax.psum(lev_terms, 'dev') / (num_dev * feat_width)  81.7 us
    all_gather x1, waiting for transfers between devices, body(): lax.all_gather(own_rows, 'rep', axis=0, tiled=True)  70.1 us
    all_to_all x1, blocking collectives, body(): lax.all_to_all(jnp.stack(jnp.split(features, lax.axis_size('dev'), axis=1...  37.5 us
    dot_general x1, matrix products, body(): jnp.dot(all_rows, all_white.T, precision=lax.Precision.HIGHEST)  32.1 us
    another operation x30, matrix products, body(): solved = jax.scipy.linalg.cho_solve((cholesky_factor, True), white_block)  25.2 us
    another operation x14, matrix products, body(): cholesky_factor = jnp.linalg.cholesky(capacitance)  22.9 us
  transfers between devices with their start and end apart: 3, of which 1 were waited for; matrix products, arithmetic and copies ran while one was open for 0% of the time, Pallas kernels for 0%

profile of v1, /device:TPU:1, one launch (start us, length us, event | category | flops | bytes accessed | tf_op | source)
XLA Modules:
  0.0 657.7 jit_solution(2649103576879779104)
XLA Ops:
  27.8 37.5 %all_to_all.20 = f32[32,8,1,2048]{3,2,1,0:T(1,128)S(1)} all-to-all(f32[32,8,1,2048]{3,2,1,0:T(1,128)S(1)} %constant_dynamic-update-slice_fusion), channel_id=1, replica_groups=mesh['dev'=32,'rep'=4] {'dev'}, dimensions={0} | all-to-all | bytes 4194304 | tf_op jit(solution)/shard_map/all_to_all | solution.py:24
  65.3 19.9 %multiply_reduce_fusion = (f32[256]{0:T(256)S(1)}, f32[256,2048]{1,0:T(8,128)}) fusion(f32[32,8,1,2048]{3,2,1,0:T(1,128)S(1)} %all_to_all.20, f32[1,2048,2048]{2,1,0:T(8,128)} %param.5), kind=kOutput, calls=%fused_computation.17 | convolution fusion | flops 12885950464 | bytes 20972544 | tf_op jit(solution)/shard_map/dot_general | solution.py:29
  91.8 81.7 %psum.7 = f32[256]{0:T(256)S(1)} all-reduce(f32[256]{0:T(256)S(1)} %get-tuple-element.60), channel_id=1, replica_groups=mesh['dev'=32,'rep'=4] {'dev'}, use_global_device_ids=true, to_apply=%region_1.0 | all-reduce | flops 256 | bytes 2048 | tf_op jit(solution)/shard_map/psum | solution.py:31
  173.5 8.0 %all-gather = f32[4,1,256]{2,1,0:T(1,128)S(1)} all-gather(f32[1,1,256]{2,1,0:T(1,128)S(1)} %bitcast.305), channel_id=1, replica_groups=mesh['dev'=32,'rep'=4] {'rep'}, dimensions={0}, use_global_device_ids=true | all-gather | bytes 5120 | tf_op jit(solution)/shard_map/all_gather | solution.py:35
  182.1 70.1 %all-gather.4.cloned.1.call-done = f32[1024,2048]{1,0:T(8,128)} async-done(((f32[256,2048]{1,0:T(8,128)}), f32[1024,2048]{1,0:T(8,128)}) %all-gather.4.cloned.1.call-update) | async-done | bytes 8388624 | tf_op jit(solution)/shard_map/all_gather | solution.py:33
  252.2 32.1 %fusion.105 = f32[1024,1024]{1,0:T(8,128)} fusion(f32[1024,2048]{1,0:T(8,128)} %all-gather.4.cloned.1.call-done, f32[1024,2048]{1,0:T(8,128)} %all-gather.6.cloned.1.call-done), kind=kOutput, calls=%fused_computation.293 | convolution fusion | flops 25769803776 | bytes 20971520 | tf_op jit(solution)/shard_map/dot_general | solution.py:38
  296.6 11.7 %cholesky.222 = f32[128,128]{1,0:T(8,128)S(1)} custom-call(f32[128,128]{1,0:T(8,128)S(1)} %cholesky.577), custom_call_target="Cholesky" | custom-call | tf_op jit(solution)/shard_map/jit(cholesky)/cholesky | solution.py:41
  310.8 9.8 %custom-call.66 = f32[1,128,128]{1,2,0:T(8,128)S(1)} custom-call(f32[1,128,128]{2,1,0:T(8,128)S(1)} %get-tuple-element.59), custom_call_target="InvertDiagBlocksLowerTriangular" | custom-call | tf_op jit(solution)/shard_map/jit(cholesky)/cholesky | solution.py:41
  324.5 11.8 %cholesky.243 = f32[128,128]{1,0:T(8,128)S(1)} custom-call(f32[128,128]{1,0:T(8,128)S(1)} %cholesky.581), custom_call_target="Cholesky" | custom-call | tf_op jit(solution)/shard_map/jit(cholesky)/cholesky | solution.py:41
  337.0 9.8 %custom-call.67 = f32[1,128,128]{1,2,0:T(8,128)S(1)} custom-call(f32[1,128,128]{2,1,0:T(8,128)S(1)} %get-tuple-element.56), custom_call_target="InvertDiagBlocksLowerTriangular" | custom-call | tf_op jit(solution)/shard_map/jit(cholesky)/cholesky | solution.py:41
  350.2 11.7 %cholesky.466 = f32[128,128]{1,0:T(8,128)S(1)} custom-call(f32[128,128]{1,0:T(8,128)S(1)} %cholesky.586), custom_call_target="Cholesky" | custom-call | tf_op jit(solution)/shard_map/jit(cholesky)/cholesky | solution.py:41
  362.5 9.8 %custom-call.68 = f32[1,128,128]{1,2,0:T(8,128)S(1)} custom-call(f32[1,128,128]{2,1,0:T(8,128)S(1)} %get-tuple-element.53), custom_call_target="InvertDiagBlocksLowerTriangular" | custom-call | tf_op jit(solution)/shard_map/jit(cholesky)/cholesky | solution.py:41
  375.8 11.9 %cholesky.485 = f32[128,128]{1,0:T(8,128)S(1)} custom-call(f32[128,128]{1,0:T(8,128)S(1)} %cholesky.591), custom_call_target="Cholesky" | custom-call | tf_op jit(solution)/shard_map/jit(cholesky)/cholesky | solution.py:41
  388.4 9.8 %custom-call.69 = f32[1,128,128]{1,2,0:T(8,128)S(1)} custom-call(f32[1,128,128]{2,1,0:T(8,128)S(1)} %get-tuple-element.50), custom_call_target="InvertDiagBlocksLowerTriangular" | custom-call | tf_op jit(solution)/shard_map/jit(cholesky)/cholesky | solution.py:41
  401.6 11.7 %cholesky.504 = f32[128,128]{1,0:T(8,128)S(1)} custom-call(f32[128,128]{1,0:T(8,128)S(1)} %cholesky.596), custom_call_target="Cholesky" | custom-call | tf_op jit(solution)/shard_map/jit(cholesky)/cholesky | solution.py:41
  413.9 10.2 %custom-call.70 = f32[1,128,128]{1,2,0:T(8,128)S(1)} custom-call(f32[1,128,128]{2,1,0:T(8,128)S(1)} %get-tuple-element.47), custom_call_target="InvertDiagBlocksLowerTriangular" | custom-call | tf_op jit(solution)/shard_map/jit(cholesky)/cholesky | solution.py:41
  427.4 11.7 %cholesky.524 = f32[128,128]{1,0:T(8,128)S(1)} custom-call(f32[128,128]{1,0:T(8,128)S(1)} %cholesky.601), custom_call_target="Cholesky" | custom-call | tf_op jit(solution)/shard_map/jit(cholesky)/cholesky | solution.py:41
  439.8 9.8 %custom-call.71 = f32[1,128,128]{1,2,0:T(8,128)S(1)} custom-call(f32[1,128,128]{2,1,0:T(8,128)S(1)} %get-tuple-element.44), custom_call_target="InvertDiagBlocksLowerTriangular" | custom-call | tf_op jit(solution)/shard_map/jit(cholesky)/cholesky | solution.py:41
  452.6 11.9 %cholesky.544 = f32[128,128]{1,0:T(8,128)S(1)} custom-call(f32[128,128]{1,0:T(8,128)S(1)} %cholesky.606), custom_call_target="Cholesky" | custom-call | tf_op jit(solution)/shard_map/jit(cholesky)/cholesky | solution.py:41
  465.1 9.8 %custom-call.72 = f32[1,128,128]{1,2,0:T(8,128)S(1)} custom-call(f32[1,128,128]{2,1,0:T(8,128)S(1)} %get-tuple-element.41), custom_call_target="InvertDiagBlocksLowerTriangular" | custom-call | tf_op jit(solution)/shard_map/jit(cholesky)/cholesky | solution.py:41
  477.6 11.7 %cholesky.562 = f32[128,128]{1,0:T(8,128)S(1)} custom-call(f32[128,128]{1,0:T(8,128)S(1)} %convolution_subtract_fusion.20), custom_call_target="Cholesky" | custom-call | tf_op jit(solution)/shard_map/jit(cholesky)/cholesky | solution.py:41
  504.2 22.6 %while.1 = (s32[]{:T(128)}, f32[1024,1024]{1,0:T(8,128)}, s32[8,2]{0,1:T(2,128)S(1)}, f32[8,128,128]{2,1,0:T(8,128)S(1)}, s32[]{:T(128)}) while((s32[]{:T(128)}, f32[1024,1024]{1,0:T(8,128)}, s32[8,2]{0,1:T(2,128)S(1)}, f32[8,128,128]{2,1,0:T(8,128)S(1)}, s32[]{:T(128)}) %tuple.61), condition=%wide.while_cond, body=%wide.while_body.sunk | while | flops 2 | bytes 131189 | solution.py:45
  526.8 78.8 %custom-call.73 = f32[8,128,128]{1,2,0:T(8,128)S(1)} custom-call(f32[8,128,128]{2,1,0:T(8,128)S(1)} %get-tuple-element.10), custom_call_target="InvertDiagBlocksLowerTriangular" | custom-call | tf_op jit(solution)/shard_map/jit(_cho_solve)/triangular_solve | solution.py:45
  632.4 16.7 %fusion.4 = f32[1,512,2048]{2,1,0:T(8,128)} fusion(f32[1,2048,2048]{2,1,0:T(8,128)} %param.5, s32[]{:T(128)S(6)} %select_n.20, f32[1024,512]{1,0:T(8,128)S(1)} %constant_dynamic-update-slice_fusion.68, f32[1024,2048]{1,0:T(8,128)S(1)} %bitcast.299), kind=kOutput, calls=%fused_computation.9 | convolution fusion | flops 12885950464 | bytes 18874372 | tf_op jit(solution)/shard_map/dot_general | solution.py:47
  (176 shorter events, 129.1 us)
Async XLA Ops:
  7.2 174.9 %all-gather.6.cloned.1.call-start = ((), (), s32[]{:S(2)}) async-start(), calls=%async_computation.3 | async-start | bytes 10485760 | tf_op jit(solution)/shard_map/all_gather | solution.py:34
  85.2 167.0 %all-gather.4.cloned.1.call-start = ((), (), s32[]{:S(2)}) async-start(), calls=%async_computation.2 | async-start | bytes 10485760 | tf_op jit(solution)/shard_map/all_gather | solution.py:33
  87.5 94.6 %all-to-all-start.1 = ((f32[32,8,1,2048]{3,1,2,0:T(8,128)}), f32[32,8,1,2048]{3,1,2,0:T(8,128)S(1)}, u32[]{:S(2)}, u32[]{:S(2)}) async-start(f32[32,8,1,2048]{3,1,2,0:T(8,128)} %bitcast.35), calls=%async_computation.1 | async-start | bytes 4194304 | tf_op jit(solution)/shard_map/all_to_all | solution.py:48
  294.6 2.0 copy-start.1
  607.0 3.9 copy-start
  628.4 3.6 slice-start
  630.1 2.3 slice-start.1
Sparse Core Ops, SparseCore 0:
  85.3 80.5 all-gather.5
  168.1 84.0 all-gather.3
